TPU v7x, 32 devices: a whole 2x2x4 slice. The times are simulated.
32 devices in a mesh: dp: 16 (over z, y, x), rep: 2 (over core).
Axes of the slice: x: 2, y: 2, z: 4, core: 2. Of those that a mesh axis runs over, the one named last changes fastest.
Arguments:
- queries: bfloat16 [24576, 256], P(('dp', 'rep')), may hold values from -100 to 100
- candidates: bfloat16 [24576, 256], P(('dp', 'rep')), may hold values from -6 to 6
- bucket: int32 [24576, 1], P(('dp', 'rep')), may hold values from 0 to 15, as said below
Outputs:
- query_loss: float32 [24576], P(('dp', 'rep'))
- bucket_loss: float32 [16], P('dp')
Inputs may be any that keep to these rules, and one draw needn't show every extreme that they name: The 768 rows of one device name any bucket at most 96 times; on some device some bucket is named exactly 96 times; a bucket may be named by no row at all.
All inputs are finite; a program needn't handle non-finite values.
Results may differ from a plain program's by a relative error of at most 0.0003.
Values may be sent and summed in bfloat16 or wider, within the bound.
A program may use at most 64 MiB of HBM per device.

v0:
```python
import math

import jax
import jax.numpy as jnp
from jax import lax
from jax.sharding import PartitionSpec as P

score_scale = 0.0625
neg_large = -1e30


def block_stats(qrows, crows, cvalid):
    count = qrows.shape[0]
    blocksize = math.gcd(count, 512)
    columns = crows.shape[0]
    colsize = math.gcd(columns, 2048)
    col_blocks = crows.reshape(columns // colsize, colsize, crows.shape[1])
    valid_blocks = cvalid.reshape(columns // colsize, colsize)

    def one_block(block):

        def step(carry, item):
            top, total = carry
            cpiece, vpiece = item
            scores = (
                lax.dot_general(
                    block, cpiece, (((1,), (1,)), ((), ())), preferred_element_type=jnp.float32
                )
                * score_scale
            )
            scores = jnp.where(vpiece[None, :] > 0, scores, neg_large)
            new_top = jnp.maximum(top, jnp.max(scores, axis=1))
            total = total * jnp.exp(top - new_top) + jnp.sum(
                jnp.exp(scores - new_top[:, None]), axis=1
            )
            return ((new_top, total), None)

        start = (
            jnp.full((block.shape[0],), neg_large, jnp.float32),
            jnp.zeros((block.shape[0],), jnp.float32),
        )
        (top, total), _ = lax.scan(step, start, (col_blocks, valid_blocks))
        return (top, total)

    top, total = lax.map(one_block, qrows.reshape(count // blocksize, blocksize, qrows.shape[1]))
    return (top.reshape(-1), total.reshape(-1))


def shards(queries, candidates, bucket):
    peers = lax.axis_size("dp")
    rows_here = queries.shape[0]
    width = queries.shape[1]
    cap = max(2, 2 * rows_here // peers)
    slots = peers * cap
    owner = bucket[:, 0]
    onehot = (owner[:, None] == jnp.arange(peers, dtype=jnp.int32)[None, :]).astype(jnp.int32)
    rank = jnp.sum(jnp.cumsum(onehot, axis=0) * onehot, axis=1) - 1
    slot = owner * cap + rank
    send_q = (
        jnp.zeros((slots, width), jnp.bfloat16).at[slot].set(queries).reshape(peers, cap, width)
    )
    send_c = (
        jnp.zeros((slots, width), jnp.bfloat16).at[slot].set(candidates).reshape(peers, cap, width)
    )
    send_v = jnp.zeros((slots,), jnp.bfloat16).at[slot].set(1.0).reshape(peers, cap)
    recv_q, recv_c, recv_v = (
        lax.all_to_all(send_q, "dp", split_axis=0, concat_axis=0, tiled=True),
        lax.all_to_all(send_c, "dp", split_axis=0, concat_axis=0, tiled=True),
        lax.all_to_all(send_v, "dp", split_axis=0, concat_axis=0, tiled=True),
    )
    recv_q = recv_q.reshape(slots, width)
    recv_c = recv_c.reshape(slots, width)
    recv_v = recv_v.reshape(slots)
    whole_c, whole_v = (
        lax.all_gather(recv_c, "rep", axis=0, tiled=True),
        lax.all_gather(recv_v, "rep", axis=0, tiled=True),
    )
    top, total = block_stats(recv_q, whole_c, whole_v)
    count = jnp.sum(whole_v.astype(jnp.float32))
    lse = top + jnp.log(total)
    positive = (
        jnp.sum(recv_q.astype(jnp.float32) * recv_c.astype(jnp.float32), axis=1) * score_scale
    )
    count_safe = jnp.maximum(count, 1.0)
    loss = jnp.where(recv_v.astype(jnp.float32) > 0, lse - jnp.log(count_safe) - positive, 0.0)
    returned = lax.all_to_all(
        loss.reshape(peers, cap), "dp", split_axis=0, concat_axis=0, tiled=True
    ).reshape(-1)
    query_loss = returned[slot]
    loss_total = lax.psum(jnp.sum(loss), "rep")
    bucket_loss = (loss_total / count_safe).reshape(1)
    return (query_loss, bucket_loss)


def solution(mesh):
    in_specs = (P(("dp", "rep"), None), P(("dp", "rep"), None), P(("dp", "rep"), None))
    out_specs = (P(("dp", "rep")), P("dp"))
    return jax.shard_map(shards, mesh=mesh, in_specs=in_specs, out_specs=out_specs, check_vma=False)
```

profile of v0, /device:TPU:0, one launch (start us, length us, event | category | flops | bytes accessed | tf_op | source)
XLA Modules:
  0.0 135.0 jit_solution(16670390724771292902)
XLA Ops:
  7.9 1.7 %reduce-window.6 = s32[16,6,128]{2,0,1:T(8,128)S(1)} reduce-window(s32[16,6,128]{2,0,1:T(8,128)S(1)} %fusion.12, s32[]{:T(128)} %constant.37.clone.1), window={size=1x1x128 pad=0_0x0_0x127_0}, to_apply=%region_0.0 | reduce-window | flops 1560576 | bytes 98308 | tf_op jit(solution)/shard_map/reduce-window
  10.7 8.6 %scatter_custom_fusion = bf16[1536]{0:T(1024)(128)(2,1)S(1)} fusion(s32[768]{0:T(1024)S(1)} %fusion.14, bf16[768]{0:T(1024)(128)(2,1)S(1)} %broadcast.99, bf16[]{:T(256)} %constant.13.clone.1), kind=kCustom, calls=%fused_computation.39 | custom fusion | bytes 3074 | tf_op jit(solution)/shard_map/scatter | solution.py:65
  20.0 8.3 %all-to-all-start = ((bf16[16,1,96]{2,1,0:T(2,128)(2,1)}), bf16[16,1,96]{2,1,0:T(2,128)(2,1)S(1)}, u32[]{:S(2)}, u32[]{:S(2)}) async-start(bf16[16,1,96]{2,1,0:T(2,128)(2,1)} %all_to_all.21), calls=%async_computation | async-start | bytes 16384 | tf_op jit(solution)/shard_map/all_to_all | solution.py:69
  28.4 6.7 %scatter_custom_fusion.2 = bf16[1536,256]{1,0:T(8,128)(2,1)} fusion(s32[768]{0:T(1024)S(1)} %fusion.14, bf16[768,256]{1,0:T(8,128)(2,1)} %param.8, bf16[]{:T(256)} %constant.13.clone.1), kind=kCustom, calls=%fused_computation.17 | custom fusion | bytes 786944 | tf_op jit(solution)/shard_map/scatter | solution.py:63
  35.7 6.3 %all-to-all-start.2 = ((bf16[16,96,256]{2,1,0:T(8,128)(2,1)}), bf16[16,96,256]{2,1,0:T(8,128)(2,1)S(1)}, u32[]{:S(2)}, u32[]{:S(2)}) async-start(bf16[16,96,256]{2,1,0:T(8,128)(2,1)} %bitcast.6), calls=%async_computation.2 | async-start | bytes 1572864 | tf_op jit(solution)/shard_map/all_to_all | solution.py:68
  42.0 6.7 %scatter_custom_fusion.1 = bf16[1536,256]{1,0:T(8,128)(2,1)} fusion(s32[768]{0:T(1024)S(1)} %fusion.14, bf16[768,256]{1,0:T(8,128)(2,1)} %param.7, bf16[]{:T(256)} %constant.13.clone.1), kind=kCustom, calls=%fused_computation.19 | custom fusion | bytes 786944 | tf_op jit(solution)/shard_map/scatter | solution.py:60
  48.7 12.4 %all-to-all-done.2 = bf16[16,96,256]{2,1,0:T(8,128)(2,1)S(1)} async-done(((bf16[16,96,256]{2,1,0:T(8,128)(2,1)}), bf16[16,96,256]{2,1,0:T(8,128)(2,1)S(1)}, u32[]{:S(2)}, u32[]{:S(2)}) %all-to-all-start.2) | async-done | bytes 786464 | tf_op jit(solution)/shard_map/all_to_all | solution.py:68
  61.1 5.0 %all-to-all-start.1 = ((bf16[16,96,256]{2,1,0:T(8,128)(2,1)}), bf16[16,96,256]{2,1,0:T(8,128)(2,1)S(1)}, u32[]{:S(2)}, u32[]{:S(2)}) async-start(bf16[16,96,256]{2,1,0:T(8,128)(2,1)} %bitcast.4), calls=%async_computation.1 | async-start | bytes 1572864 | tf_op jit(solution)/shard_map/all_to_all | solution.py:67
  67.0 2.0 %all-gather = bf16[2,1,1536]{2,1,0:T(2,128)(2,1)S(1)} all-gather(bf16[1,1,1536]{2,1,0:T(2,128)(2,1)S(1)} %reshape.160), channel_id=1, replica_groups=mesh['dp'=16,'rep'=2] {'rep'}, dimensions={0}, use_global_device_ids=true | all-gather | bytes 9216 | tf_op jit(solution)/shard_map/all_gather | solution.py:76
  70.3 14.4 %all-to-all-done.1 = bf16[16,96,256]{2,1,0:T(8,128)(2,1)S(1)} async-done(((bf16[16,96,256]{2,1,0:T(8,128)(2,1)}), bf16[16,96,256]{2,1,0:T(8,128)(2,1)S(1)}, u32[]{:S(2)}, u32[]{:S(2)}) %all-to-all-start.1) | async-done | bytes 786464 | tf_op jit(solution)/shard_map/all_to_all | solution.py:67
  86.2 19.8 %while.26 = (s32[]{:T(128)}, f32[3,512]{1,0:T(4,128)S(1)}, f32[3,512]{1,0:T(4,128)S(1)}, bf16[3,512,256]{2,1,0:T(8,128)(2,1)S(1)}, bf16[3,1024]{1,0:T(4,128)(2,1...) while((s32[]{:T(128)}, f32[3,512]{1,0:T(4,128)S(1)}, ...), condition=%wide.region_11.12_spmd, body=%wide.region_6.11_spmd.sunk | while | flops 272111104 | bytes 5545265 | solution.py:45
  86.3 6.4 %while.27 = (s32[]{:T(128)}, f32[512]{0:T(512)S(1)}, f32[512]{0:T(512)S(1)}, bf16[3,1024]{1,0:T(4,128)(2,1)S(1)}, bf16[3,1024,256]{2,1,0:T(8,128)(2,1)}, /*index=5*/bf16[512,256]{1,0:T(8,128)(2,1)S(1)}, s32[]{:T(128)}, s32[]{:T(128)}) while((s32[]{:T(128)}, f32[512]{0:T(512)S(1)}, f32[512]{0:T(512)S(1)}, ...), condition=%wide.region_10.10_spmd.clone, body=%wide.region_7.9_spmd.clone.sunk | while | flops 272111104 | bytes 5012592 | solution.py:42
  88.5 1.5 %fusion.22 = (f32[512]{0:T(512)S(1)}, f32[1024,512]{1,0:T(8,128)S(1)}) fusion(pred[1024]{0:T(1024)(128)(4,1)S(1)} %compare_reduce_fusion.2, bf16[512,256]{1,0:T(8,128)(2,1)S(1)} %get-tuple-element.235, bf16[3,1024,256]{2,1,0:T(8,128)(2,1)} %get-tuple-element.234, s32[]{:T(128)S(6)} %copy.23), kind=kOutput, calls=%fused_computation.6.clone.1 | convolution fusion | flops 270007808 | bytes 2886660 | tf_op jit(solution)/shard_map/while/body/eval_jaxpr/while/body/eval_jaxpr/dot_general | solution.py:26
  90.6 1.5 %fusion.22 = (f32[512]{0:T(512)S(1)}, f32[1024,512]{1,0:T(8,128)S(1)}) fusion(pred[1024]{0:T(1024)(128)(4,1)S(1)} %compare_reduce_fusion.2, bf16[512,256]{1,0:T(8,128)(2,1)S(1)} %get-tuple-element.235, bf16[3,1024,256]{2,1,0:T(8,128)(2,1)} %get-tuple-element.234, s32[]{:T(128)S(6)} %copy.23), kind=kOutput, calls=%fused_computation.6.clone.1 | convolution fusion | flops 270007808 | bytes 2886660 | tf_op jit(solution)/shard_map/while/body/eval_jaxpr/while/body/eval_jaxpr/dot_general | solution.py:26
  92.9 6.4 %while.27 = (s32[]{:T(128)}, f32[512]{0:T(512)S(1)}, f32[512]{0:T(512)S(1)}, bf16[3,1024]{1,0:T(4,128)(2,1)S(1)}, bf16[3,1024,256]{2,1,0:T(8,128)(2,1)}, /*index=5*/bf16[512,256]{1,0:T(8,128)(2,1)S(1)}, s32[]{:T(128)}, s32[]{:T(128)}) while((s32[]{:T(128)}, f32[512]{0:T(512)S(1)}, f32[512]{0:T(512)S(1)}, ...), condition=%wide.region_10.10_spmd.clone, body=%wide.region_7.9_spmd.clone.sunk | while | flops 272111104 | bytes 5012592 | solution.py:42
  92.9 1.5 %fusion.22 = (f32[512]{0:T(512)S(1)}, f32[1024,512]{1,0:T(8,128)S(1)}) fusion(pred[1024]{0:T(1024)(128)(4,1)S(1)} %compare_reduce_fusion.2, bf16[512,256]{1,0:T(8,128)(2,1)S(1)} %get-tuple-element.235, bf16[3,1024,256]{2,1,0:T(8,128)(2,1)} %get-tuple-element.234, s32[]{:T(128)S(6)} %copy.23), kind=kOutput, calls=%fused_computation.6.clone.1 | convolution fusion | flops 270007808 | bytes 2886660 | tf_op jit(solution)/shard_map/while/body/eval_jaxpr/while/body/eval_jaxpr/dot_general | solution.py:26
  95.1 1.5 %fusion.22 = (f32[512]{0:T(512)S(1)}, f32[1024,512]{1,0:T(8,128)S(1)}) fusion(pred[1024]{0:T(1024)(128)(4,1)S(1)} %compare_reduce_fusion.2, bf16[512,256]{1,0:T(8,128)(2,1)S(1)} %get-tuple-element.235, bf16[3,1024,256]{2,1,0:T(8,128)(2,1)} %get-tuple-element.234, s32[]{:T(128)S(6)} %copy.23), kind=kOutput, calls=%fused_computation.6.clone.1 | convolution fusion | flops 270007808 | bytes 2886660 | tf_op jit(solution)/shard_map/while/body/eval_jaxpr/while/body/eval_jaxpr/dot_general | solution.py:26
  99.5 6.4 %while.27 = (s32[]{:T(128)}, f32[512]{0:T(512)S(1)}, f32[512]{0:T(512)S(1)}, bf16[3,1024]{1,0:T(4,128)(2,1)S(1)}, bf16[3,1024,256]{2,1,0:T(8,128)(2,1)}, /*index=5*/bf16[512,256]{1,0:T(8,128)(2,1)S(1)}, s32[]{:T(128)}, s32[]{:T(128)}) while((s32[]{:T(128)}, f32[512]{0:T(512)S(1)}, f32[512]{0:T(512)S(1)}, ...), condition=%wide.region_10.10_spmd.clone, body=%wide.region_7.9_spmd.clone.sunk | while | flops 272111104 | bytes 5012592 | solution.py:42
  99.5 1.5 %fusion.22 = (f32[512]{0:T(512)S(1)}, f32[1024,512]{1,0:T(8,128)S(1)}) fusion(pred[1024]{0:T(1024)(128)(4,1)S(1)} %compare_reduce_fusion.2, bf16[512,256]{1,0:T(8,128)(2,1)S(1)} %get-tuple-element.235, bf16[3,1024,256]{2,1,0:T(8,128)(2,1)} %get-tuple-element.234, s32[]{:T(128)S(6)} %copy.23), kind=kOutput, calls=%fused_computation.6.clone.1 | convolution fusion | flops 270007808 | bytes 2886660 | tf_op jit(solution)/shard_map/while/body/eval_jaxpr/while/body/eval_jaxpr/dot_general | solution.py:26
  101.7 1.5 %fusion.22 = (f32[512]{0:T(512)S(1)}, f32[1024,512]{1,0:T(8,128)S(1)}) fusion(pred[1024]{0:T(1024)(128)(4,1)S(1)} %compare_reduce_fusion.2, bf16[512,256]{1,0:T(8,128)(2,1)S(1)} %get-tuple-element.235, bf16[3,1024,256]{2,1,0:T(8,128)(2,1)} %get-tuple-element.234, s32[]{:T(128)S(6)} %copy.23), kind=kOutput, calls=%fused_computation.6.clone.1 | convolution fusion | flops 270007808 | bytes 2886660 | tf_op jit(solution)/shard_map/while/body/eval_jaxpr/while/body/eval_jaxpr/dot_general | solution.py:26
  107.4 5.0 %all-to-all-start.3 = ((f32[16,1,96]{2,1,0:T(1,128)}), f32[16,1,96]{2,1,0:T(1,128)S(1)}, u32[]{:S(2)}, u32[]{:S(2)}) async-start(f32[16,1,96]{2,1,0:T(1,128)} %bitcast.10), calls=%async_computation.3 | async-start | bytes 16384 | tf_op jit(solution)/shard_map/all_to_all | solution.py:86
  112.4 3.1 %psum.7 = f32[]{:T(128)} all-reduce(f32[]{:T(128)} %get-tuple-element.115), channel_id=1, replica_groups=mesh['dp'=16,'rep'=2] {'rep'}, use_global_device_ids=true, to_apply=%region_15.16 | all-reduce | flops 1 | bytes 8 | tf_op jit(solution)/shard_map/psum | solution.py:90
  116.1 3.5 %all-to-all-done.3 = f32[16,1,96]{2,1,0:T(1,128)S(1)} async-done(((f32[16,1,96]{2,1,0:T(1,128)}), f32[16,1,96]{2,1,0:T(1,128)S(1)}, u32[]{:S(2)}, u32[]{:S(2)}) %all-to-all-start.3) | async-done | bytes 6176 | tf_op jit(solution)/shard_map/all_to_all | solution.py:86
  120.9 6.1 %gather_fusion = f32[768]{0:T(1024)} fusion(f32[1536]{0:T(1024)S(1)} %reshape.126, s32[1024]{0:T(1024)S(1)} %pad_clamp_fusion), kind=kCustom, calls=%fused_computation | custom fusion | bytes 9216 | tf_op jit(solution)/shard_map/gather | solution.py:89
  (95 shorter events, 18.8 us)
Async XLA Ops:
  20.0 15.6 %all-to-all-start = ((bf16[16,1,96]{2,1,0:T(2,128)(2,1)}), bf16[16,1,96]{2,1,0:T(2,128)(2,1)S(1)}, u32[]{:S(2)}, u32[]{:S(2)}) async-start(bf16[16,1,96]{2,1,0:T(2,128)(2,1)} %all_to_all.21), calls=%async_computation | async-start | bytes 16384 | tf_op jit(solution)/shard_map/all_to_all | solution.py:69
  35.7 25.5 %all-to-all-start.2 = ((bf16[16,96,256]{2,1,0:T(8,128)(2,1)}), bf16[16,96,256]{2,1,0:T(8,128)(2,1)S(1)}, u32[]{:S(2)}, u32[]{:S(2)}) async-start(bf16[16,96,256]{2,1,0:T(8,128)(2,1)} %bitcast.6), calls=%async_computation.2 | async-start | bytes 1572864 | tf_op jit(solution)/shard_map/all_to_all | solution.py:68
  61.1 5.0 %copy-start = (bf16[16,96,256]{2,1,0:T(8,128)(2,1)}, bf16[16,96,256]{2,1,0:T(8,128)(2,1)S(1)}, u32[]{:S(2)}) copy-start(bf16[16,96,256]{2,1,0:T(8,128)(2,1)S(1)} %all-to-all-done.2) | copy-start | bytes 2359300
  61.1 23.6 %all-to-all-start.1 = ((bf16[16,96,256]{2,1,0:T(8,128)(2,1)}), bf16[16,96,256]{2,1,0:T(8,128)(2,1)S(1)}, u32[]{:S(2)}, u32[]{:S(2)}) async-start(bf16[16,96,256]{2,1,0:T(8,128)(2,1)} %bitcast.4), calls=%async_computation.1 | async-start | bytes 1572864 | tf_op jit(solution)/shard_map/all_to_all | solution.py:67
  66.1 20.1 %all-gather.3.cloned.1.call-start = ((), (), s32[]{:S(2)}) async-start(), calls=%async_computation.4 | async-start | bytes 2359296 | tf_op jit(solution)/shard_map/all_gather | solution.py:75
  107.4 12.3 %all-to-all-start.3 = ((f32[16,1,96]{2,1,0:T(1,128)}), f32[16,1,96]{2,1,0:T(1,128)S(1)}, u32[]{:S(2)}, u32[]{:S(2)}) async-start(f32[16,1,96]{2,1,0:T(1,128)} %bitcast.10), calls=%async_computation.3 | async-start | bytes 16384 | tf_op jit(solution)/shard_map/all_to_all | solution.py:86
Sparse Core Ops, SparseCore 0:
  68.4 11.0 all-gather.2
where the time goes:
time: 136 us; the launch traced here: 135 us
  waiting for transfers between devices  31.5 us (23%)
  local copies, waits for them, and re-layouts  30.4 us (22%)
  starting transfers between devices  24.6 us (18%)
  between operations  16.7 us (12%)
  matrix products  13.8 us (10%)
  other arithmetic  12.4 us (9%)
  blocking collectives  5.09 us (4%)
    all_to_all x1, waiting for transfers between devices, shards(): lax.all_to_all(send_q, 'dp', split_axis=0, concat_axis=0, tiled=True)  14.4 us
    dot_general x9, matrix products, step(): lax.dot_general(block, cpiece, (((1,), (1,)), ((), ())), preferred_elemen...  13.8 us
    all_to_all x1, waiting for transfers between devices, shards(): lax.all_to_all(send_c, 'dp', split_axis=0, concat_axis=0, tiled=True)  12.4 us
    scatter x1, local copies, waits for them, and re-layouts, shards(): jnp.zeros((slots,), jnp.bfloat16).at[slot].set(1.0).reshape(peers, cap)  8.62 us
    all_to_all x1, starting transfers between devices, shards(): lax.all_to_all(send_v, 'dp', split_axis=0, concat_axis=0, tiled=True)  8.34 us
    scatter x1, local copies, waits for them, and re-layouts, shards(): jnp.zeros((slots, width), jnp.bfloat16).at[slot].set(queries)  6.73 us
    scatter x1, local copies, waits for them, and re-layouts, shards(): jnp.zeros((slots, width), jnp.bfloat16).at[slot].set(candidates)  6.72 us
    all_to_all x1, starting transfers between devices, shards(): lax.all_to_all(send_c, 'dp', split_axis=0, concat_axis=0, tiled=True)  6.33 us
  transfers between devices with their start and end apart: 5, of which 4 were waited for; matrix products, arithmetic and copies ran while one was open for 12% of the time, Pallas kernels for 0%

commit v1 on v0

v1 whole, which is shorter than its diff:
```python
import functools
import math

import jax
import jax.numpy as jnp
from jax import lax
from jax.experimental import pallas as pl
from jax.experimental.pallas import tpu as pltpu
from jax.sharding import PartitionSpec as P

MESH = pl.DeviceIdType.MESH
score_scale = 0.0625
neg_large = -1e30
log2e = math.log2(math.e)


def xor(a, b, n):
    out, bit = 0, 1
    while bit < n:
        out = out + bit * ((a // bit + b // bit) % 2)
        bit *= 2
    return out


def kernel(
    n, cap, b_ref, q_ref, c_ref, ql_ref, bl_ref,
    slot_buf, hot_buf, rank_buf, bias_buf, s_buf,
    qs, cs, qr, cr, co, vs, vr, vo, ls, lr, xs, xr,
    c_ss, c_rs, q_ss, q_rs, v_ss, v_rs, l_ss, l_rs, f_ss, f_rs, x_ss, x_rs,
):
    me = lax.axis_index("dp")
    rep = lax.axis_index("rep")
    partner = (me, 1 - rep)
    rows, width = q_ref.shape
    slots = n * cap

    barrier = pltpu.get_barrier_semaphore()

    def greet(k, carry):
        pl.semaphore_signal(
            barrier, inc=1, device_id=(xor(me, k, n), rep), device_id_type=MESH
        )
        return carry

    lax.fori_loop(1, n, greet, 0)
    pl.semaphore_signal(barrier, inc=1, device_id=partner, device_id_type=MESH)

    hot = (b_ref[...] == lax.broadcasted_iota(jnp.int32, (rows, n), 1)).astype(jnp.bfloat16)
    first = lax.broadcasted_iota(jnp.int32, (rows, rows), 0)
    second = lax.broadcasted_iota(jnp.int32, (rows, rows), 1)
    before = (first < second).astype(jnp.bfloat16)
    same = (first == second).astype(jnp.bfloat16)
    dims = (((0,), (0,)), ((), ()))
    ahead = lax.dot_general(hot, before, dims, preferred_element_type=jnp.float32)
    hot_t = lax.dot_general(hot, same, dims, preferred_element_type=jnp.float32)
    owner_col = lax.broadcasted_iota(jnp.int32, (n, rows), 0).astype(jnp.float32)
    rank = jnp.sum(hot_t * ahead, axis=0, keepdims=True)
    base = jnp.sum(hot_t * owner_col, axis=0, keepdims=True) * cap
    hot_buf[...] = hot_t
    rank_buf[...] = rank.astype(jnp.int32)
    slot_buf[...] = (base + rank).astype(jnp.int32)
    counts = jnp.sum(hot_t, axis=1, keepdims=True)
    vs[:, 0, :] = jnp.broadcast_to(counts, (n, 128))

    pl.semaphore_wait(barrier, n)

    def remote(src, dst, ss, rs, device):
        return pltpu.make_async_remote_copy(
            src_ref=src, dst_ref=dst, send_sem=ss, recv_sem=rs,
            device_id=device, device_id_type=MESH,
        )

    def v_copy(o):
        return remote(vs.at[o], vr.at[me], v_ss.at[o], v_rs.at[me], (o, rep))

    def c_copy(o):
        return remote(cs.at[o], cr.at[me], c_ss.at[o], c_rs.at[me], (o, rep))

    def q_copy(o):
        return remote(qs.at[o], qr.at[me], q_ss.at[o], q_rs.at[me], (o, rep))

    def l_copy(o):
        return remote(ls.at[o], lr.at[me], l_ss.at[o], l_rs.at[me], (o, rep))

    def f_copy(o):
        return remote(cr.at[o], co.at[o], f_ss.at[o], f_rs.at[o], partner)

    def v_from(o):
        return remote(vs.at[me], vr.at[o], v_ss.at[o], v_rs.at[o], (o, rep))

    def c_from(o):
        return remote(cs.at[me], cr.at[o], c_ss.at[o], c_rs.at[o], (o, rep))

    def q_from(o):
        return remote(qs.at[me], qr.at[o], q_ss.at[o], q_rs.at[o], (o, rep))

    def l_from(o):
        return remote(ls.at[me], lr.at[o], l_ss.at[o], l_rs.at[o], (o, rep))

    within = lax.broadcasted_iota(jnp.int32, (cap, rows), 0)

    def pick(o, x_ref):
        chosen = (slot_buf[...] == within + o * cap).astype(jnp.bfloat16)
        return jnp.dot(chosen, x_ref[...], preferred_element_type=jnp.float32).astype(
            jnp.bfloat16
        )

    cs[xor(me, n - 1, n)] = pick(xor(me, n - 1, n), c_ref)

    def pack_c(t, carry):
        k = n - 1 - t
        nxt = xor(me, k - 1, n)
        cs[nxt] = pick(nxt, c_ref)
        o = xor(me, k, n)
        c_copy(o).start()
        v_copy(o).start()
        return carry

    lax.fori_loop(0, n - 1, pack_c, 0)
    cr[me] = cs[me]
    vr[me] = vs[me]

    qs[xor(me, n - 1, n)] = pick(xor(me, n - 1, n), q_ref)

    def pack_q(t, carry):
        k = n - 1 - t
        nxt = xor(me, k - 1, n)
        qs[nxt] = pick(nxt, q_ref)
        q_copy(xor(me, k, n)).start()
        return carry

    lax.fori_loop(0, n - 1, pack_q, 0)
    qr[me] = qs[me]
    f_copy(me).start()

    def forward(t, carry):
        o = xor(me, n - 1 - t, n)
        c_from(o).wait_recv()
        f_copy(o).start()
        v_from(o).wait_recv()
        return carry

    lax.fori_loop(0, n - 1, forward, 0)
    v_forward = remote(vr, vo, x_ss.at[0], x_rs.at[0], partner)
    v_forward.start()
    v_forward.wait_recv()

    spread = (
        lax.broadcasted_iota(jnp.int32, (n, slots), 0)
        == lax.broadcasted_iota(jnp.int32, (n, slots), 1) // cap
    ).astype(jnp.bfloat16)
    place = lax.broadcasted_iota(jnp.int32, (1, slots), 1) % cap
    mine, other = vr[:, 0, :], vo[:, 0, :]
    for half, held in enumerate((mine, other)):
        number = lax.dot_general(
            held.astype(jnp.bfloat16), spread, dims, preferred_element_type=jnp.float32
        )[0:1]
        bias_buf[:, half * slots : (half + 1) * slots] = jnp.where(
            place.astype(jnp.float32) < number, 0.0, neg_large
        )
    count = jnp.sum(mine, axis=0, keepdims=True) + jnp.sum(other, axis=0, keepdims=True)
    count_safe = jnp.maximum(count, 1.0)
    log_count = jnp.log(count_safe)

    def landed(t, carry):
        f_copy(xor(me, n - 1 - t, n)).wait_recv()
        return carry

    lax.fori_loop(0, n, landed, 0)

    chunk = math.gcd(slots, 256)
    row_at = lax.broadcasted_iota(jnp.int32, (cap, 128), 0)
    lane_at = lax.broadcasted_iota(jnp.int32, (cap, 128), 1)
    diagonal = row_at == lane_at
    row_number = row_at.astype(jnp.float32)

    def block_loss(j):
        block = qr[j]
        top = jnp.full((cap, 128), neg_large, jnp.float32)
        for half, held in enumerate((cr, co)):
            flat = held.reshape(slots, width)
            for start in range(0, slots, chunk):
                at = half * slots + start
                scores = lax.dot_general(
                    block, flat[start : start + chunk, :],
                    (((1,), (1,)), ((), ())), preferred_element_type=jnp.float32,
                ) + bias_buf[:, at : at + chunk]
                s_buf[:, at : at + chunk] = scores
                for lane in range(0, chunk, 128):
                    top = jnp.maximum(top, scores[:, lane : lane + 128])
        peak = jnp.max(top, axis=1, keepdims=True)
        wide = jnp.broadcast_to(peak, (cap, 128))
        total = jnp.zeros((cap, 128), jnp.float32)
        for at in range(0, 2 * slots, 128):
            total = total + jnp.exp2((s_buf[:, at : at + 128] - wide) * (score_scale * log2e))
        lse = peak * score_scale + jnp.log(jnp.sum(total, axis=1, keepdims=True))
        positive = score_scale * jnp.sum(
            block.astype(jnp.float32) * cr[j].astype(jnp.float32), axis=1, keepdims=True
        )
        loss = (lse - positive) - log_count
        keep = jnp.logical_and(diagonal, row_number < vr[j])
        return jnp.sum(jnp.where(keep, loss, 0.0), axis=0, keepdims=True)

    mine_row = block_loss(me)
    lr[me] = mine_row

    def step(t, total):
        j = xor(me, n - 1 - t, n)
        q_from(j).wait_recv()
        row = block_loss(j)
        ls[j] = row
        total = total + row
        xs[...] = total
        l_copy(j).start()
        return total

    total = lax.fori_loop(0, n - 1, step, mine_row)
    x_copy = remote(xs, xr, x_ss.at[1], x_rs.at[1], partner)
    x_copy.start()

    def close(t, carry):
        o = xor(me, n - 1 - t, n)
        c_copy(o).wait_send()
        q_copy(o).wait_send()
        v_copy(o).wait_send()
        l_copy(o).wait_send()
        f_copy(o).wait_send()
        l_from(o).wait_recv()
        return carry

    lax.fori_loop(0, n - 1, close, 0)
    f_copy(me).wait_send()
    v_forward.wait_send()

    spread_loss = lax.dot_general(
        lr[:, 0, :], hot_buf[...], dims,
        precision=lax.Precision.HIGHEST, preferred_element_type=jnp.float32,
    )
    here = lax.broadcasted_iota(jnp.int32, (128, rows), 0) == rank_buf[...]
    ql_ref[...] = jnp.sum(jnp.where(here, spread_loss, 0.0), axis=0, keepdims=True)
    x_copy.wait()
    summed = jnp.sum(total + xr[...], axis=1, keepdims=True)
    bl_ref[...] = summed / count_safe


def shards(queries, candidates, bucket):
    n = lax.axis_size("dp")
    rows, width = queries.shape
    cap = max(2, 2 * rows // n)
    cap = (cap + 15) // 16 * 16
    slots = n * cap
    bf16, f32 = jnp.bfloat16, jnp.float32
    vmem = pl.BlockSpec(memory_space=pltpu.VMEM)
    dma = pltpu.SemaphoreType.DMA
    query_loss, bucket_loss = pl.pallas_call(
        functools.partial(kernel, n, cap),
        out_shape=(
            jax.ShapeDtypeStruct((1, rows), f32),
            jax.ShapeDtypeStruct((1, 128), f32),
        ),
        in_specs=[vmem] * 3,
        out_specs=(vmem, vmem),
        scratch_shapes=[
            pltpu.VMEM((1, rows), jnp.int32),
            pltpu.VMEM((n, rows), f32),
            pltpu.VMEM((1, rows), jnp.int32),
            pltpu.VMEM((1, 2 * slots), f32),
            pltpu.VMEM((cap, 2 * slots), f32),
            pltpu.VMEM((n, cap, width), bf16),
            pltpu.VMEM((n, cap, width), bf16),
            pltpu.VMEM((n, cap, width), bf16),
            pltpu.VMEM((n, cap, width), bf16),
            pltpu.VMEM((n, cap, width), bf16),
            pltpu.VMEM((n, 1, 128), f32),
            pltpu.VMEM((n, 1, 128), f32),
            pltpu.VMEM((n, 1, 128), f32),
            pltpu.VMEM((n, 1, 128), f32),
            pltpu.VMEM((n, 1, 128), f32),
            pltpu.VMEM((1, 128), f32),
            pltpu.VMEM((1, 128), f32),
        ]
        + [dma((n,))] * 10
        + [dma((2,))] * 2,
        compiler_params=pltpu.CompilerParams(collective_id=0, has_side_effects=True),
        name="bucket_loss",
    )(bucket, queries, candidates)
    return query_loss.reshape(rows), bucket_loss[0, :1]


def solution(mesh):
    in_specs = (P(("dp", "rep"), None), P(("dp", "rep"), None), P(("dp", "rep"), None))
    out_specs = (P(("dp", "rep")), P("dp"))
    return jax.shard_map(shards, mesh=mesh, in_specs=in_specs, out_specs=out_specs, check_vma=False)
```

time: 136 us -> 62 us (0.46)
  Pallas kernels: 0 us -> 57 us
  waiting for transfers between devices: 31.5 us -> 0 us
  local copies, waits for them, and re-layouts: 30.4 us -> 2.35 us
  starting transfers between devices: 24.6 us -> 0 us
  between operations: 16.7 us -> 1.81 us
  matrix products: 13.8 us -> 0 us
  other arithmetic: 12.4 us -> 0.6 us
  blocking collectives: 5.09 us -> 0 us
    pallas_call x0 -> x1, Pallas kernels: none -> 57 us  [shards(): pl.pallas_call(functools.partial(kernel, n, cap), out_shape=(jax.ShapeDty...]
    all_to_all x4 -> x0, waiting for transfers between devices: 30.9 us -> none  [the longest x1 14.4 us: shards(): lax.all_to_all(send_q, 'dp', split_axis=0, concat_axis=0, tiled=True)]
    all_to_all x4 -> x0, starting transfers between devices: 24.6 us -> none  [the longest x1 8.34 us: shards(): lax.all_to_all(send_v, 'dp', split_axis=0, concat_axis=0, tiled=True)]
    scatter x3 -> x0, local copies, waits for them, and re-layouts: 22.1 us -> none  [the longest x1 8.62 us: shards(): jnp.zeros((slots,), jnp.bfloat16).at[slot].set(1.0).reshape(peers, cap)]
    dot_general x9 -> x0, matrix products: 13.8 us -> none  [step(): lax.dot_general(block, cpiece, (((1,), (1,)), ((), ())), preferred_elemen...]
    reduce_sum x13 -> x0, other arithmetic: 7.36 us -> none  [the longest x9 4.56 us: step(): jnp.sum(jnp.exp(scores - new_top[:, None]), axis=1)]
    gather x1 -> x0, local copies, waits for them, and re-layouts: 6.14 us -> none  [shards(): query_loss = returned[slot]]
    psum x1 -> x0, blocking collectives: 3.11 us -> none  [shards(): loss_total = lax.psum(jnp.sum(loss), 'rep')]
  transfers between devices with their start and end apart: 5 -> 0, of which waited for: 4 -> 0; matrix products, arithmetic and copies ran while one was open for 12% -> 0% of each run, Pallas kernels for 0% -> 0%
where the time goes in v1:
time: 62 us; the launch traced here: 61.8 us
  Pallas kernels  57 us (92%)
  local copies, waits for them, and re-layouts  2.35 us (4%)
  between operations  1.81 us (3%)
    pallas_call x1, Pallas kernels, shards(): pl.pallas_call(functools.partial(kernel, n, cap), out_shape=(jax.ShapeDty...  57 us
    unnamed x5, local copies, waits for them, and re-layouts  2.35 us

profile of v1, /device:TPU:0, one launch (start us, length us, event | category | flops | bytes accessed | tf_op | source)
XLA Modules:
  0.0 61.8 jit_solution(17294168273200503217)
XLA Ops:
  0.6 1.6 %copy.5.b_ref = s32[768,1]{1,0:T(8,128)} copy(s32[768,1]{0,1:T(1,128)} %param.5) | data formatting | bytes 6144 | tf_op args[2]
  2.2 57.0 %bucket_loss.1 = (f32[1,768]{1,0:T(1,128)}, f32[1,128]{1,0:T(1,128)}) custom-call(s32[768,1]{1,0:T(8,128)} %copy.5.b_ref, bf16[768,256]{1,0:T(8,128)(2,1)} %q_ref.1, bf16[768,256]{1,0:T(8,128)(2,1)} %c_ref.1), custom_call_target="tpu_custom_call" | custom-call | tf_op jit(solution)/shard_map/bucket_loss/pallas_call | solution.py:255
  59.3 0.0 copy-start
  59.3 0.7 %copy-done = f32[1,768]{1,0:T(1,128)S(1)} copy-done((f32[1,768]{1,0:T(1,128)S(1)}, f32[1,768]{1,0:T(1,128)}, u32[]{:S(2)}) %copy-start) | copy-done | bytes 3096
  60.0 0.0 copy-start.1
  60.0 0.6 reduce
  60.6 0.1 copy-done.1
Async XLA Ops:
  59.3 0.7 %copy-start = (f32[1,768]{1,0:T(1,128)S(1)}, f32[1,768]{1,0:T(1,128)}, u32[]{:S(2)}) copy-start(f32[1,768]{1,0:T(1,128)} %get-tuple-element.4) | copy-start | bytes 9220
  60.0 0.7 %copy-start.1 = (f32[1,128]{1,0:T(1,128)S(1)}, f32[1,128]{1,0:T(1,128)}, u32[]{:S(2)}) copy-start(f32[1,128]{1,0:T(1,128)} %get-tuple-element.5) | copy-start | bytes 1540

commit v2 on v1

v2 whole, which is shorter than its diff:
```python
import functools
import math

import jax
import jax.numpy as jnp
from jax import lax
from jax.experimental import pallas as pl
from jax.experimental.pallas import tpu as pltpu
from jax.sharding import PartitionSpec as P

MESH = pl.DeviceIdType.MESH
score_scale = 0.0625
neg_large = -1e30
log2e = math.log2(math.e)


def xor(a, b, n):
    out, bit = 0, 1
    while bit < n:
        out = out + bit * ((a // bit + b // bit) % 2)
        bit *= 2
    return out


def kernel(
    n, cap, group, b_ref, q_ref, c_ref, ql_ref, bl_ref,
    slot_buf, hot_buf, rank_buf, bias_buf, s_buf,
    qs, cs, qr, cr, co, vs, vr, vo, ls, lr, xs, xr,
    c_ss, c_rs, q_ss, q_rs, v_ss, v_rs, l_ss, l_rs, f_ss, f_rs, x_ss, x_rs,
):
    me = lax.axis_index("dp")
    rep = lax.axis_index("rep")
    partner = (me, 1 - rep)
    rows, width = q_ref.shape
    slots = n * cap
    lanes = group * cap
    groups = n // group
    quarter = n // 4
    zone = me // quarter
    middle = (zone * (3 - zone)) // 2

    barrier = pltpu.get_barrier_semaphore()

    def greet(k, carry):
        pl.semaphore_signal(
            barrier, inc=1, device_id=(xor(me, k, n), rep), device_id_type=MESH
        )
        return carry

    lax.fori_loop(1, n, greet, 0)
    pl.semaphore_signal(barrier, inc=1, device_id=partner, device_id_type=MESH)

    owner_col = lax.broadcasted_iota(jnp.int32, (n, rows), 0)
    chosen = owner_col == b_ref[...]
    hot = jnp.where(chosen, 1.0, 0.0)
    before = (
        lax.broadcasted_iota(jnp.int32, (rows, rows), 0)
        < lax.broadcasted_iota(jnp.int32, (rows, rows), 1)
    ).astype(jnp.bfloat16)
    dims = (((0,), (0,)), ((), ()))
    ahead = jnp.dot(hot.astype(jnp.bfloat16), before, preferred_element_type=jnp.float32)
    rank = jnp.sum(hot * ahead, axis=0, keepdims=True).astype(jnp.int32)
    hot_buf[...] = hot
    rank_buf[...] = rank
    slot_buf[...] = b_ref[...] * cap + rank
    vs[:, 0, :] = jnp.broadcast_to(jnp.sum(hot, axis=1, keepdims=True), (n, lanes))

    def remote(src, dst, ss, rs, device):
        return pltpu.make_async_remote_copy(
            src_ref=src, dst_ref=dst, send_sem=ss, recv_sem=rs,
            device_id=device, device_id_type=MESH,
        )

    def v_copy(o):
        return remote(vs.at[o], vr.at[me], v_ss.at[o], v_rs.at[me], (o, rep))

    def c_copy(o):
        return remote(cs.at[o], cr.at[me], c_ss.at[o], c_rs.at[me], (o, rep))

    def q_copy(o):
        return remote(qs.at[o], qr.at[me], q_ss.at[o], q_rs.at[me], (o, rep))

    def l_copy(o):
        return remote(ls.at[o // group], lr.at[me], l_ss.at[o], l_rs.at[me], (o, rep))

    def f_copy(o):
        return remote(cr.at[o], co.at[o], f_ss.at[o], f_rs.at[o], partner)

    def v_from(o):
        return remote(vs.at[me], vr.at[o], v_ss.at[o], v_rs.at[o], (o, rep))

    def c_from(o):
        return remote(cs.at[me], cr.at[o], c_ss.at[o], c_rs.at[o], (o, rep))

    def q_from(o):
        return remote(qs.at[me], qr.at[o], q_ss.at[o], q_rs.at[o], (o, rep))

    def l_from(o):
        return remote(ls.at[0], lr.at[o], l_ss.at[o], l_rs.at[o], (o, rep))

    within = lax.broadcasted_iota(jnp.int32, (cap, rows), 0)

    def pick(o, x_ref):
        taken = (slot_buf[...] == within + o * cap).astype(jnp.bfloat16)
        return jnp.dot(taken, x_ref[...], preferred_element_type=jnp.float32).astype(
            jnp.bfloat16
        )

    def peer(t):
        near = quarter + (t + middle * quarter) % (3 * quarter)
        inside = (t + 1) % quarter
        apart = t // (3 * quarter)
        return xor(me, near * (1 - apart) + inside * apart, n)

    def arrival(u, size):
        return size + (u + middle * 2 * size) % (3 * size)

    cs[peer(0)] = pick(peer(0), c_ref)
    pl.semaphore_wait(barrier, n)

    def pack_c(t, carry):
        nxt = peer(t + 1)
        cs[nxt] = pick(nxt, c_ref)
        o = peer(t)
        c_copy(o).start()
        v_copy(o).start()
        return carry

    lax.fori_loop(0, n - 1, pack_c, 0)
    cr[me] = cs[me]
    vr[me] = vs[me]

    qs[peer(0)] = pick(peer(0), q_ref)

    def pack_q(t, carry):
        nxt = peer(t + 1)
        qs[nxt] = pick(nxt, q_ref)
        q_copy(peer(t)).start()
        return carry

    lax.fori_loop(0, n - 1, pack_q, 0)
    qr[me] = qs[me]
    f_copy(me).start()

    row_at = lax.broadcasted_iota(jnp.int32, (cap, lanes), 0)
    lane_at = lax.broadcasted_iota(jnp.int32, (cap, lanes), 1)
    row_number = row_at.astype(jnp.float32)

    def fill_bias(number, at):
        bias_buf[pl.ds(pl.multiple_of(at, cap), cap), :] = jnp.where(
            row_number < number, 0.0, neg_large
        )

    def forward(o):
        c_from(o).wait_recv()
        f_copy(o).start()
        v_from(o).wait_recv()

    lax.fori_loop(1, quarter, lambda k, c: (forward(xor(me, k, n)), c)[1], 0)
    lax.fori_loop(
        0, 3 * quarter, lambda u, c: (forward(xor(me, arrival(u, quarter), n)), c)[1], 0
    )
    v_forward = remote(vr, vo, x_ss.at[0], x_rs.at[0], partner)
    v_forward.start()
    lax.fori_loop(0, n, lambda j, c: (fill_bias(vr[j], j * cap), c)[1], 0)
    v_forward.wait_recv()
    lax.fori_loop(0, n, lambda j, c: (fill_bias(vo[j], (n + j) * cap), c)[1], 0)
    count = jnp.sum(vr[:, 0, :], axis=0, keepdims=True) + jnp.sum(
        vo[:, 0, :], axis=0, keepdims=True
    )
    count_safe = jnp.maximum(count, 1.0)
    log_count = jnp.log(count_safe)
    lax.fori_loop(0, n, lambda j, c: (f_copy(j).wait_recv(), c)[1], 0)

    chunk = math.gcd(slots, 256)
    one_row = lax.broadcasted_iota(jnp.int32, (1, lanes), 1)

    def group_loss(p):
        block = qr[pl.ds(p * group, group)].reshape(lanes, width)
        top = jnp.full((8, lanes), neg_large, jnp.float32)
        for half, held in enumerate((cr, co)):
            flat = held.reshape(slots, width)
            for start in range(0, slots, chunk):
                at = half * slots + start
                scores = lax.dot_general(
                    flat[start : start + chunk, :], block,
                    (((1,), (1,)), ((), ())), preferred_element_type=jnp.float32,
                ) + bias_buf[at : at + chunk, :]
                s_buf[at : at + chunk, :] = scores
                top = jnp.maximum(top, jnp.max(scores.reshape(chunk // 8, 8, lanes), axis=0))
        peak = jnp.max(top, axis=0, keepdims=True)
        total = jnp.zeros((8, lanes), jnp.float32)
        for at in range(0, 2 * slots, chunk):
            powers = jnp.exp2((s_buf[at : at + chunk, :] - peak) * (score_scale * log2e))
            total = total + jnp.sum(powers.reshape(chunk // 8, 8, lanes), axis=0)
        lse = peak * score_scale + jnp.log(jnp.sum(total, axis=0, keepdims=True))
        positive = jnp.zeros((1, lanes), jnp.float32)
        keep = jnp.zeros((1, lanes), jnp.float32)
        for g in range(group):
            j = p * group + g
            own = s_buf[pl.ds(pl.multiple_of(j * cap, cap), cap), :]
            positive = positive + jnp.sum(
                jnp.where(row_at == lane_at - g * cap, own, 0.0), axis=0, keepdims=True
            )
            place = one_row - g * cap
            here = jnp.logical_and(place >= 0, place.astype(jnp.float32) < vr[j])
            here = jnp.logical_and(here, place < cap)
            keep = jnp.where(here, 1.0, keep)
        loss = (lse - positive * score_scale) - log_count
        return jnp.where(keep > 0.0, loss, 0.0)

    def step(m, total):
        p = xor(me // group, m, groups)
        for g in range(group):
            j = p * group + g

            @pl.when(j != me)
            def _():
                q_from(j).wait_recv()

        row = group_loss(p)
        ls[p] = row
        total = total + row
        xs[...] = total
        for g in range(group):
            j = p * group + g

            @pl.when(j != me)
            def _():
                l_copy(j).start()

        return total

    part = groups // 4
    total = lax.fori_loop(0, part, step, jnp.zeros((1, lanes), jnp.float32))
    total = lax.fori_loop(0, 3 * part, lambda u, c: step(arrival(u, part), c), total)
    lr[me] = ls[me // group]
    x_copy = remote(xs, xr, x_ss.at[1], x_rs.at[1], partner)
    x_copy.start()

    def close(t, carry):
        o = xor(me, n - 1 - t, n)
        c_copy(o).wait_send()
        q_copy(o).wait_send()
        v_copy(o).wait_send()
        l_copy(o).wait_send()
        f_copy(o).wait_send()
        l_from(o).wait_recv()
        return carry

    lax.fori_loop(0, n - 1, close, 0)
    f_copy(me).wait_send()
    v_forward.wait_send()

    spread_loss = lax.dot_general(
        lr[:, 0, :], hot_buf[...], dims,
        precision=lax.Precision.HIGHEST, preferred_element_type=jnp.float32,
    )
    mine = lax.broadcasted_iota(jnp.int32, (lanes, rows), 0) == rank_buf[...] + (me % group) * cap
    ql_ref[...] = jnp.sum(jnp.where(mine, spread_loss, 0.0), axis=0)
    x_copy.wait()
    summed = jnp.sum(total + xr[...], axis=1, keepdims=True)
    bl_ref[...] = (summed / count_safe)[:, :128]


def shards(queries, candidates, bucket):
    n = lax.axis_size("dp")
    rows, width = queries.shape
    cap = max(2, 2 * rows // n)
    cap = (cap + 15) // 16 * 16
    group = 1
    while 2 * group * cap <= 256 and n % (8 * group) == 0:
        group *= 2
    slots, lanes = n * cap, group * cap
    bf16, f32 = jnp.bfloat16, jnp.float32
    vmem = pl.BlockSpec(memory_space=pltpu.VMEM)
    dma = pltpu.SemaphoreType.DMA
    query_loss, bucket_loss = pl.pallas_call(
        functools.partial(kernel, n, cap, group),
        out_shape=(
            jax.ShapeDtypeStruct((rows,), f32),
            jax.ShapeDtypeStruct((1, 128), f32),
        ),
        in_specs=[vmem] * 3,
        out_specs=(vmem, vmem),
        scratch_shapes=[
            pltpu.VMEM((1, rows), jnp.int32),
            pltpu.VMEM((n, rows), f32),
            pltpu.VMEM((1, rows), jnp.int32),
            pltpu.VMEM((2 * slots, lanes), f32),
            pltpu.VMEM((2 * slots, lanes), f32),
        ]
        + [pltpu.VMEM((n, cap, width), bf16)] * 5
        + [pltpu.VMEM((n, 1, lanes), f32)] * 3
        + [pltpu.VMEM((n // group, 1, lanes), f32), pltpu.VMEM((n, 1, lanes), f32)]
        + [pltpu.VMEM((1, lanes), f32)] * 2
        + [dma((n,))] * 10
        + [dma((2,))] * 2,
        compiler_params=pltpu.CompilerParams(collective_id=0, has_side_effects=True),
        name="bucket_loss",
    )(bucket.reshape(1, rows), queries, candidates)
    return query_loss, bucket_loss[0, :1]


def solution(mesh):
    in_specs = (P(("dp", "rep"), None), P(("dp", "rep"), None), P(("dp", "rep"), None))
    out_specs = (P(("dp", "rep")), P("dp"))
    return jax.shard_map(shards, mesh=mesh, in_specs=in_specs, out_specs=out_specs, check_vma=False)
```

time: 62 us -> 60.4 us (0.974)
  local copies, waits for them, and re-layouts: 2.35 us -> 1.31 us
    unnamed x5, local copies, waits for them, and re-layouts: 2.35 us -> 1.31 us
where the time goes in v2:
time: 60.4 us; the launch traced here: 60.2 us
  Pallas kernels  57.1 us (95%)
  between operations  1.81 us (3%)
  local copies, waits for them, and re-layouts  1.31 us (2%)
    pallas_call x1, Pallas kernels, shards(): pl.pallas_call(functools.partial(kernel, n, cap, group), out_shape=(jax.S...  57.1 us
    unnamed x5, local copies, waits for them, and re-layouts  1.31 us

profile of v2, /device:TPU:0, one launch (start us, length us, event | category | flops | bytes accessed | tf_op | source)
XLA Modules:
  0.0 60.2 jit_solution(17873819071891018951)
XLA Ops:
  0.6 57.1 %bucket_loss.1 = (f32[768]{0:T(1024)}, f32[1,128]{1,0:T(1,128)}) custom-call(s32[1,768]{1,0:T(1,128)} %bitcast.3, bf16[768,256]{1,0:T(8,128)(2,1)} %q_ref.1, bf16[768,256]{1,0:T(8,128)(2,1)} %c_ref.1), custom_call_target="tpu_custom_call" | custom-call | tf_op jit(solution)/shard_map/bucket_loss/pallas_call | solution.py:278
  57.8 0.0 copy-start
  57.8 0.7 %copy-done = f32[768]{0:T(1024)S(1)} copy-done((f32[768]{0:T(1024)S(1)}, f32[768]{0:T(1024)}, u32[]{:S(2)}) %copy-start) | copy-done | bytes 3096
  58.4 0.0 copy-start.1
  58.4 0.6 copy.7
  59.0 0.0 copy-done.1
Async XLA Ops:
  57.8 0.7 %copy-start = (f32[768]{0:T(1024)S(1)}, f32[768]{0:T(1024)}, u32[]{:S(2)}) copy-start(f32[768]{0:T(1024)} %get-tuple-element.8) | copy-start | bytes 9220
  58.4 0.6 %copy-start.1 = (f32[1,128]{1,0:T(1,128)S(1)}, f32[1,128]{1,0:T(1,128)}, u32[]{:S(2)}) copy-start(f32[1,128]{1,0:T(1,128)} %get-tuple-element.5) | copy-start | bytes 1540

commit v3 on v2

--- a/solution.py
+++ b/solution.py
@@ -23,10 +23,10 @@
 
 
 def kernel(
-    n, cap, group, b_ref, q_ref, c_ref, ql_ref, bl_ref,
+    n, cap, group, b_hbm, q_hbm, c_hbm, ql_ref, bl_ref, b_ref, q_ref, c_ref,
     slot_buf, hot_buf, rank_buf, bias_buf, s_buf,
     qs, cs, qr, cr, co, vs, vr, vo, ls, lr, xs, xr,
-    c_ss, c_rs, q_ss, q_rs, v_ss, v_rs, l_ss, l_rs, f_ss, f_rs, x_ss, x_rs,
+    c_ss, c_rs, q_ss, q_rs, v_ss, v_rs, l_ss, l_rs, f_ss, f_rs, x_ss, x_rs, in_sem,
 ):
     me = lax.axis_index("dp")
     rep = lax.axis_index("rep")
@@ -49,6 +49,14 @@
 
     lax.fori_loop(1, n, greet, 0)
     pl.semaphore_signal(barrier, inc=1, device_id=partner, device_id_type=MESH)
+
+    b_in = pltpu.make_async_copy(b_hbm, b_ref, in_sem.at[0])
+    c_in = pltpu.make_async_copy(c_hbm, c_ref, in_sem.at[1])
+    q_in = pltpu.make_async_copy(q_hbm, q_ref, in_sem.at[2])
+    b_in.start()
+    c_in.start()
+    q_in.start()
+    b_in.wait()
 
     owner_col = lax.broadcasted_iota(jnp.int32, (n, rows), 0)
     chosen = owner_col == b_ref[...]
@@ -107,14 +115,12 @@
         )
 
     def peer(t):
-        near = quarter + (t + middle * quarter) % (3 * quarter)
-        inside = (t + 1) % quarter
-        apart = t // (3 * quarter)
-        return xor(me, near * (1 - apart) + inside * apart, n)
+        return xor(me, n - 1 - t, n)
 
     def arrival(u, size):
-        return size + (u + middle * 2 * size) % (3 * size)
-
+        return 4 * size - 1 - (u + (1 - middle) * 2 * size) % (3 * size)
+
+    c_in.wait()
     cs[peer(0)] = pick(peer(0), c_ref)
     pl.semaphore_wait(barrier, n)
 
@@ -130,6 +136,7 @@
     cr[me] = cs[me]
     vr[me] = vs[me]
 
+    q_in.wait()
     qs[peer(0)] = pick(peer(0), q_ref)
 
     def pack_q(t, carry):
@@ -278,12 +285,15 @@
     query_loss, bucket_loss = pl.pallas_call(
         functools.partial(kernel, n, cap, group),
         out_shape=(
-            jax.ShapeDtypeStruct((rows,), f32),
-            jax.ShapeDtypeStruct((1, 128), f32),
+            pltpu.VMEM((rows,), f32),
+            pltpu.VMEM((1, 128), f32),
         ),
-        in_specs=[vmem] * 3,
+        in_specs=[pl.BlockSpec(memory_space=pl.ANY)] * 3,
         out_specs=(vmem, vmem),
         scratch_shapes=[
+            pltpu.VMEM((1, rows), jnp.int32),
+            pltpu.VMEM((rows, width), bf16),
+            pltpu.VMEM((rows, width), bf16),
             pltpu.VMEM((1, rows), jnp.int32),
             pltpu.VMEM((n, rows), f32),
             pltpu.VMEM((1, rows), jnp.int32),
@@ -295,7 +305,8 @@
         + [pltpu.VMEM((n // group, 1, lanes), f32), pltpu.VMEM((n, 1, lanes), f32)]
         + [pltpu.VMEM((1, lanes), f32)] * 2
         + [dma((n,))] * 10
-        + [dma((2,))] * 2,
+        + [dma((2,))] * 2
+        + [dma((3,))],
         compiler_params=pltpu.CompilerParams(collective_id=0, has_side_effects=True),
         name="bucket_loss",
     )(bucket.reshape(1, rows), queries, candidates)

time: 60.4 us -> 51.9 us (0.86)
  Pallas kernels: 57.1 us -> 49.3 us
  local copies, waits for them, and re-layouts: 1.31 us -> 0.6 us
    pallas_call x1, Pallas kernels: 57.1 us -> 49.3 us  [shards(): pl.pallas_call(functools.partial(kernel, n, cap, group), out_shape=(pltpu...]
    unnamed x5 -> x1, local copies, waits for them, and re-layouts: 1.31 us -> 0.6 us
where the time goes in v3:
time: 51.9 us; the launch traced here: 51.7 us
  Pallas kernels  49.3 us (95%)
  between operations  1.8 us (3%)
  local copies, waits for them, and re-layouts  0.6 us (1%)
    pallas_call x1, Pallas kernels, shards(): pl.pallas_call(functools.partial(kernel, n, cap, group), out_shape=(pltpu...  49.3 us

profile of v3, /device:TPU:0, one launch (start us, length us, event | category | flops | bytes accessed | tf_op | source)
XLA Modules:
  0.0 51.7 jit_solution(13889402408366328010)
XLA Ops:
  0.6 49.3 %bucket_loss.1 = (f32[768]{0:T(1024)S(1)}, f32[1,128]{1,0:T(1,128)S(1)}) custom-call(s32[1,768]{1,0:T(1,128)} %bitcast.4, bf16[768,256]{1,0:T(8,128)(2,1)} %q_hbm.1, bf16[768,256]{1,0:T(8,128)(2,1)} %c_hbm.1), custom_call_target="tpu_custom_call" | custom-call | tf_op jit(solution)/shard_map/bucket_loss/pallas_call | solution.py:285
  49.9 0.6 %copy.7 = f32[768]{0:T(1024)} copy(f32[768]{0:T(1024)S(1)} %get-tuple-element.6) | data formatting | bytes 6144

commit v4 on v3

--- a/solution.py
+++ b/solution.py
@@ -43,7 +43,7 @@
 
     def greet(k, carry):
         pl.semaphore_signal(
-            barrier, inc=1, device_id=(xor(me, k, n), rep), device_id_type=MESH
+            barrier, inc=1, device_id=((me + k) % n, rep), device_id_type=MESH
         )
         return carry
 
@@ -178,6 +178,17 @@
     count_safe = jnp.maximum(count, 1.0)
     log_count = jnp.log(count_safe)
     lax.fori_loop(0, n, lambda j, c: (f_copy(j).wait_recv(), c)[1], 0)
+
+    def sent(t, carry):
+        o = (me + 1 + t) % n
+        c_copy(o).wait_send()
+        v_copy(o).wait_send()
+        f_copy(o).wait_send()
+        return carry
+
+    lax.fori_loop(0, n - 1, sent, 0)
+    f_copy(me).wait_send()
+    v_forward.wait_send()
 
     chunk = math.gcd(slots, 256)
     one_row = lax.broadcasted_iota(jnp.int32, (1, lanes), 1)
@@ -246,18 +257,13 @@
     x_copy.start()
 
     def close(t, carry):
-        o = xor(me, n - 1 - t, n)
-        c_copy(o).wait_send()
+        o = (me + 1 + t) % n
         q_copy(o).wait_send()
-        v_copy(o).wait_send()
         l_copy(o).wait_send()
-        f_copy(o).wait_send()
         l_from(o).wait_recv()
         return carry
 
     lax.fori_loop(0, n - 1, close, 0)
-    f_copy(me).wait_send()
-    v_forward.wait_send()
 
     spread_loss = lax.dot_general(
         lr[:, 0, :], hot_buf[...], dims,

time: 51.9 us -> 51.6 us (level)
  no operation moved by 1% of the time
where the time goes in v4:
time: 51.6 us; the launch traced here: 51.2 us
  Pallas kernels  48.8 us (95%)
  between operations  1.8 us (3%)
  local copies, waits for them, and re-layouts  0.6 us (1%)
    pallas_call x1, Pallas kernels, shards(): pl.pallas_call(functools.partial(kernel, n, cap, group), out_shape=(pltpu...  48.8 us

profile of v4, /device:TPU:0, one launch (start us, length us, event | category | flops | bytes accessed | tf_op | source)
XLA Modules:
  0.0 51.2 jit_solution(16635639283874293773)
XLA Ops:
  0.6 48.8 %bucket_loss.1 = (f32[768]{0:T(1024)S(1)}, f32[1,128]{1,0:T(1,128)S(1)}) custom-call(s32[1,768]{1,0:T(1,128)} %bitcast.4, bf16[768,256]{1,0:T(8,128)(2,1)} %q_hbm.1, bf16[768,256]{1,0:T(8,128)(2,1)} %c_hbm.1), custom_call_target="tpu_custom_call" | custom-call | tf_op jit(solution)/shard_map/bucket_loss/pallas_call | solution.py:291
  49.5 0.6 %copy.7 = f32[768]{0:T(1024)} copy(f32[768]{0:T(1024)S(1)} %get-tuple-element.6) | data formatting | bytes 6144
